TPU v7x, 256 devices: a whole 4x4x8 slice. The times are simulated.
256 devices in a mesh: group: 4 (over x), leaf: 64 (over z, y, core).
Axes of the slice: x: 4, y: 4, z: 8, core: 2. Of those that a mesh axis runs over, the one named last changes fastest.
Arguments:
- right_sides: float32 [16, 1048576], P(None, ('group', 'leaf')), may hold values from -6 to 6
- near_blocks: float32 [16384, 8, 4096], P(('group', 'leaf')), may hold values from -0.375 to 0.375
- near_source: int32 [16384, 8], P(('group', 'leaf')), may hold values from 0 to 16383, as said below
- near_count: int32 [16384], P(('group', 'leaf')), may hold values from 1 to 8
- basis: float32 [16384, 2048], P(('group', 'leaf')), may hold values from -0.75 to 0.75
- leaf_source: int32 [16384, 8], P(('group', 'leaf')), may hold values from 0 to 16383
- leaf_coupling: float32 [16384, 8, 1024], P(('group', 'leaf')), may hold values from -0.375 to 0.375
- leaf_transfer: float32 [16384, 1024], P(('group', 'leaf')), may hold values from -1 to 1
- cluster_source: int32 [1024, 8], P(('group', 'leaf')), may hold values from 0 to 255
- cluster_coupling: float32 [1024, 8, 1024], P(('group', 'leaf')), may hold values from -0.09375 to 0.09375
- cluster_transfer: float32 [1024, 1024], P(('group', 'leaf')), may hold values from -1 to 1
- group_coupling: float32 [4, 4, 1024], P('group'), may hold values from -0.0078125 to 0.0078125
Outputs:
- applied: float32 [16, 1048576], P(None, ('group', 'leaf'))
Inputs may be any that keep to these rules, and one draw needn't show every extreme that they name: near_source[t, j] and leaf_source[t, j] name a leaf held by the same device as t or by the device just before or after it in the order of devices.
All inputs are finite; a program needn't handle non-finite values.
Results may differ from a plain program's by a relative error of at most 0.0001.
Values sent between devices are 32-bit elements; how exact they have to be, the bound alone decides.
No kernel may reach another device: no remote copies, remote signals or barrier semaphores. Data moves between devices by JAX's collectives and lax.ppermute only.
A program may use at most 128 MiB of HBM per device.

v0:
```python
import jax
import jax.numpy as jnp
from jax import lax
from jax.sharding import PartitionSpec as P

LEAF = 64
K = 32
RHS = 16
FAR0 = 8
FAR1 = 8
highest_precision = lax.Precision.HIGHEST


def extended(value, sides, width):
    for axis, dim in sides:
        size, length = (lax.axis_size(axis), value.shape[dim])
        up = [(i, (i + 1) % size) for i in range(size - 1)]
        down = [(j, i) for i, j in up]
        last = lax.slice_in_dim(value, length - width, length, axis=dim)
        leading = lax.slice_in_dim(value, 0, width, axis=dim)
        before = lax.ppermute(last, axis, up)
        after = lax.ppermute(leading, axis, down)
        value = jnp.concatenate([before, value, after], axis=dim)
    return value


def per_device(
    right_sides,
    near_blocks,
    near_source,
    near_count,
    basis,
    leaf_source,
    leaf_coupling,
    leaf_transfer,
    cluster_source,
    cluster_coupling,
    cluster_transfer,
    group_coupling,
):
    leaves_here = near_blocks.shape[0]
    clusters_here = cluster_coupling.shape[0]
    ngroups = lax.axis_size("group")
    device = lax.axis_index(("group", "leaf"))
    blocks = right_sides.reshape(RHS, leaves_here, LEAF).transpose(1, 0, 2)
    bases = basis.reshape(leaves_here, K, LEAF)
    leaf_coef = jnp.einsum("tka,tra->tkr", bases, blocks, precision=highest_precision)
    coef_rows = leaf_coef.transpose(2, 0, 1).reshape(RHS, leaves_here * K)
    point_ext = extended(right_sides, ((("group", "leaf"), 1),), leaves_here * LEAF)
    coef_ext = extended(coef_rows, ((("group", "leaf"), 1),), leaves_here * K)
    window_start = (device - 1) * leaves_here
    near_local = near_source - window_start
    point_blocks = point_ext.reshape(RHS, 3 * leaves_here, LEAF).transpose(1, 0, 2)
    busiest = jnp.max(near_count)

    def near_step(slot_index, running):
        picked = jnp.take(point_blocks, near_local[:, slot_index], axis=0)
        slab = lax.dynamic_index_in_dim(near_blocks, slot_index, axis=1, keepdims=False).reshape(
            leaves_here, LEAF, LEAF
        )
        live = (near_count > slot_index).astype(jnp.float32)
        term = jnp.einsum("tab,trb->tra", slab, picked, precision=highest_precision)
        return running + term * live[:, None, None]

    near_total = lax.fori_loop(
        0, busiest, near_step, jnp.zeros((leaves_here, RHS, LEAF), jnp.float32)
    )
    coef_blocks = coef_ext.reshape(RHS, 3 * leaves_here, K)
    picked_coef = jnp.take(coef_blocks, leaf_source - window_start, axis=1)
    leaf_far = jnp.einsum(
        "tjkl,rtjl->tkr",
        leaf_coupling.reshape(leaves_here, FAR0, K, K),
        picked_coef,
        precision=highest_precision,
    )
    transfers = leaf_transfer.reshape(leaves_here, K, K)
    lifted = jnp.einsum("tkl,tlr->tkr", transfers, leaf_coef, precision=highest_precision)
    cluster_coef = lifted.reshape(clusters_here, leaves_here // clusters_here, K, RHS).sum(axis=1)
    cluster_rows = cluster_coef.reshape(clusters_here, K * RHS)
    couplings = cluster_coupling.reshape(clusters_here, FAR1, K, K)
    shard_rows = lax.all_gather(cluster_rows, "leaf", axis=0, tiled=True)
    onehot = (cluster_source[:, :, None] == jnp.arange(shard_rows.shape[0])[None, None, :]).astype(
        jnp.float32
    )
    selected = jnp.einsum("ujn,nm->ujm", onehot, shard_rows, precision=highest_precision)
    selected = selected.reshape(clusters_here, FAR1, K, RHS)
    cluster_far = jnp.einsum("ujkl,ujlr->ukr", couplings, selected, precision=highest_precision)
    upper = cluster_transfer.reshape(clusters_here, K, K)
    projected = jnp.einsum("ukl,ulr->ukr", upper, cluster_coef, precision=highest_precision)
    projected_sum = projected.sum(axis=0).reshape(1, K * RHS)
    group_sum = lax.psum(projected_sum, "leaf")
    all_groups = lax.all_gather(group_sum, "group", axis=0, tiled=True)
    group_field = jnp.einsum(
        "hkl,hlr->kr",
        group_coupling.reshape(ngroups, K, K),
        all_groups.reshape(ngroups, K, RHS),
        precision=highest_precision,
    )
    cluster_field = cluster_far + jnp.einsum(
        "ulk,lr->ukr", upper, group_field, precision=highest_precision
    )
    spread_cluster = jnp.repeat(cluster_field, leaves_here // clusters_here, axis=0)
    leaf_field = leaf_far + jnp.einsum(
        "tlk,tlr->tkr", transfers, spread_cluster, precision=highest_precision
    )
    total = near_total + jnp.einsum("tka,tkr->tra", bases, leaf_field, precision=highest_precision)
    return total.transpose(1, 0, 2).reshape(RHS, leaves_here * LEAF)


def solution(mesh):
    in_specs = (
        P(None, ("group", "leaf")),
        P(("group", "leaf"), None, None),
        P(("group", "leaf"), None),
        P(("group", "leaf")),
        P(("group", "leaf"), None),
        P(("group", "leaf"), None),
        P(("group", "leaf"), None, None),
        P(("group", "leaf"), None),
        P(("group", "leaf"), None),
        P(("group", "leaf"), None, None),
        P(("group", "leaf"), None),
        P("group", None, None),
    )
    out_specs = P(None, ("group", "leaf"))
    return jax.shard_map(
        per_device, mesh=mesh, in_specs=in_specs, out_specs=out_specs, check_vma=False
    )
```

profile of v0, /device:TPU:0, one launch (start us, length us, event | category | flops | bytes accessed | tf_op | source)
XLA Modules:
  0.0 376.4 jit_solution(737260132806493097)
XLA Ops:
  0.0 1.4 collective-permute-start.1
  1.4 3.7 collective-permute-start
  5.2 1.1 reshape.73
  6.3 1.5 reshape.72
  7.8 2.0 fusion.15
  10.0 0.9 reshape.74
  10.9 1.3 collective-permute-start.3
  12.2 3.7 collective-permute-start.2
  16.1 0.9 copy.85
  17.0 1.7 bitcast_reduce_fusion
  18.9 60.3 %all-gather = f32[64,4,512]{2,1,0:T(4,128)S(1)} all-gather(f32[1,4,512]{2,1,0:T(4,128)S(1)} %reshape.105), channel_id=1, replica_groups=mesh['group'=4,'leaf'=64] {'leaf'}, dimensions={0}, use_global_device_ids=true | all-gather | bytes 532480 | tf_op jit(solution)/shard_map/all_gather | solution.py:81
  79.2 1.0 reshape.112
  80.2 1.4 fusion.18
  81.8 1.1 reshape.80
  83.3 126.7 %psum.7 = f32[1,512]{1,0:T(1,128)S(1)} all-reduce(f32[1,512]{1,0:T(1,128)S(1)} %reshape.82), channel_id=1, replica_groups=mesh['group'=4,'leaf'=64] {'leaf'}, use_global_device_ids=true, to_apply=%region_4.5 | all-reduce | flops 512 | bytes 4096 | tf_op jit(solution)/shard_map/psum | solution.py:91
  209.9 11.2 %all-gather.1 = f32[4,1,512]{2,1,0:T(1,128)S(1)} all-gather(f32[1,1,512]{2,1,0:T(1,128)S(1)} %bitcast.75), channel_id=1, replica_groups=mesh['group'=4,'leaf'=64] {'group'}, dimensions={0}, use_global_device_ids=true | all-gather | bytes 10240 | tf_op jit(solution)/shard_map/all_gather | solution.py:92
  221.4 1.0 convolution_bitcast_fusion.1
  222.9 3.8 %copy.82 = f32[64,8,1024]{0,2,1:T(8,128)} copy(f32[64,8,1024]{2,1,0:T(8,128)} %param.20) | data formatting | bytes 4194304 | tf_op args[6]
  226.7 9.1 %copy.83 = f32[64,8,32,32]{3,2,1,0:T(8,128)} copy(f32[64,8,32,32]{0,3,2,1:T(8,128)} %bitcast.67) | data formatting | bytes 4194304 | tf_op jit(solution)/shard_map/reshape | solution.py:72
  236.8 1.1 concatenate.13
  237.9 1.2 copy.80
  239.0 1.1 concatenate.12
  240.4 1.1 pad_maximum_fusion
  241.6 3.1 gather_fusion.1
  244.6 10.6 %fusion.10 = f32[64,16,32]{2,1,0:T(8,128)S(1)} fusion(f32[64,8,32,32]{3,2,1,0:T(8,128)} %copy.83, f32[64,8,16,32]{3,2,1,0:T(8,128)} %bitcast.68, pred[64,8]{1,0:T(8,128)(4,1)S(1)} %copy.76), kind=kOutput, calls=%fused_computation.19 | convolution fusion | flops 100925440 | bytes 3277312 | tf_op jit(solution)/shard_map/tjkl,rtjl->tkr/dot_general | solution.py:70
  255.3 1.8 convolution_add_fusion.1
  257.1 1.0 pad_maximum_fusion.1
  258.7 2.1 copy.74
  260.8 0.8 broadcast_in_dim.31
  261.6 111.1 %while.10 = (s32[]{:T(128)}, f32[64,16,64]{2,1,0:T(8,128)}, s32[]{:T(128)}, s32[64,8]{0,1:T(8,128)S(1)}, f32[192,16,64]{2,1,0:T(8,128)}, /*index=5*/f32[64,8,409...) while((s32[]{:T(128)}, f32[64,16,64]{2,1,0:T(8,128)}, s32[]{:T(128)}, ...), condition=%wide.region_2.0_spmd, body=%wide.region_1.2_spmd.sunk | while | flops 50529796 | bytes 8656923 | solution.py:65
  262.4 4.4 %constant_dynamic-slice_fusion.2 = f32[64,1,4096]{2,1,0:T(1,128)S(1)} fusion(f32[64,8,4096]{2,1,0:T(8,128)} %get-tuple-element.170, s32[]{:T(128)S(6)} %select_n.43), kind=kLoop, calls=%fused_computation.11.clone.1 | loop fusion | bytes 2097156 | tf_op jit(solution)/shard_map/while/body/jit(dynamic_index_in_dim)/dynamic_slice | solution.py:58
  267.5 0.8 reshape.124
  268.4 2.0 gather_fusion
  270.4 5.3 %fusion.45 = f32[64,16,64]{2,1,0:T(8,128)} fusion(f32[64,16,64]{2,1,0:T(8,128)} %get-tuple-element.156, f32[64,64,64]{2,1,0:T(8,128)S(1)} %reshape.124, f32[64,16,64]{2,1,0:T(8,128)S(1)} %gather_fusion, f32[64]{0:T(128)S(1)} %compare_convert_fusion.2, pred[64]{0:T(512)(128)(4,1)S(1)} %get-tuple-element.144), kind=kOutput, calls=%fused_computation.3.clone.1 | convolution fusion | flops 50528256 | bytes 1835328 | tf_op jit(solution)/shard_map/while/body/tab,trb->tra/dot_general | solution.py:62
  276.2 4.4 %constant_dynamic-slice_fusion.2 = f32[64,1,4096]{2,1,0:T(1,128)S(1)} fusion(f32[64,8,4096]{2,1,0:T(8,128)} %get-tuple-element.170, s32[]{:T(128)S(6)} %select_n.43), kind=kLoop, calls=%fused_computation.11.clone.1 | loop fusion | bytes 2097156 | tf_op jit(solution)/shard_map/while/body/jit(dynamic_index_in_dim)/dynamic_slice | solution.py:58
  281.3 0.8 reshape.124
  282.2 2.0 gather_fusion
  284.2 5.3 %fusion.45 = f32[64,16,64]{2,1,0:T(8,128)} fusion(f32[64,16,64]{2,1,0:T(8,128)} %get-tuple-element.156, f32[64,64,64]{2,1,0:T(8,128)S(1)} %reshape.124, f32[64,16,64]{2,1,0:T(8,128)S(1)} %gather_fusion, f32[64]{0:T(128)S(1)} %compare_convert_fusion.2, pred[64]{0:T(512)(128)(4,1)S(1)} %get-tuple-element.144), kind=kOutput, calls=%fused_computation.3.clone.1 | convolution fusion | flops 50528256 | bytes 1835328 | tf_op jit(solution)/shard_map/while/body/tab,trb->tra/dot_general | solution.py:62
  290.0 4.4 %constant_dynamic-slice_fusion.2 = f32[64,1,4096]{2,1,0:T(1,128)S(1)} fusion(f32[64,8,4096]{2,1,0:T(8,128)} %get-tuple-element.170, s32[]{:T(128)S(6)} %select_n.43), kind=kLoop, calls=%fused_computation.11.clone.1 | loop fusion | bytes 2097156 | tf_op jit(solution)/shard_map/while/body/jit(dynamic_index_in_dim)/dynamic_slice | solution.py:58
  295.1 0.8 reshape.124
  295.9 2.0 gather_fusion
  298.0 5.3 %fusion.45 = f32[64,16,64]{2,1,0:T(8,128)} fusion(f32[64,16,64]{2,1,0:T(8,128)} %get-tuple-element.156, f32[64,64,64]{2,1,0:T(8,128)S(1)} %reshape.124, f32[64,16,64]{2,1,0:T(8,128)S(1)} %gather_fusion, f32[64]{0:T(128)S(1)} %compare_convert_fusion.2, pred[64]{0:T(512)(128)(4,1)S(1)} %get-tuple-element.144), kind=kOutput, calls=%fused_computation.3.clone.1 | convolution fusion | flops 50528256 | bytes 1835328 | tf_op jit(solution)/shard_map/while/body/tab,trb->tra/dot_general | solution.py:62
  303.8 4.4 %constant_dynamic-slice_fusion.2 = f32[64,1,4096]{2,1,0:T(1,128)S(1)} fusion(f32[64,8,4096]{2,1,0:T(8,128)} %get-tuple-element.170, s32[]{:T(128)S(6)} %select_n.43), kind=kLoop, calls=%fused_computation.11.clone.1 | loop fusion | bytes 2097156 | tf_op jit(solution)/shard_map/while/body/jit(dynamic_index_in_dim)/dynamic_slice | solution.py:58
  308.9 0.8 reshape.124
  309.7 2.0 gather_fusion
  311.8 5.3 %fusion.45 = f32[64,16,64]{2,1,0:T(8,128)} fusion(f32[64,16,64]{2,1,0:T(8,128)} %get-tuple-element.156, f32[64,64,64]{2,1,0:T(8,128)S(1)} %reshape.124, f32[64,16,64]{2,1,0:T(8,128)S(1)} %gather_fusion, f32[64]{0:T(128)S(1)} %compare_convert_fusion.2, pred[64]{0:T(512)(128)(4,1)S(1)} %get-tuple-element.144), kind=kOutput, calls=%fused_computation.3.clone.1 | convolution fusion | flops 50528256 | bytes 1835328 | tf_op jit(solution)/shard_map/while/body/tab,trb->tra/dot_general | solution.py:62
  317.6 4.4 %constant_dynamic-slice_fusion.2 = f32[64,1,4096]{2,1,0:T(1,128)S(1)} fusion(f32[64,8,4096]{2,1,0:T(8,128)} %get-tuple-element.170, s32[]{:T(128)S(6)} %select_n.43), kind=kLoop, calls=%fused_computation.11.clone.1 | loop fusion | bytes 2097156 | tf_op jit(solution)/shard_map/while/body/jit(dynamic_index_in_dim)/dynamic_slice | solution.py:58
  322.7 0.8 reshape.124
  323.5 2.0 gather_fusion
  325.5 5.3 %fusion.45 = f32[64,16,64]{2,1,0:T(8,128)} fusion(f32[64,16,64]{2,1,0:T(8,128)} %get-tuple-element.156, f32[64,64,64]{2,1,0:T(8,128)S(1)} %reshape.124, f32[64,16,64]{2,1,0:T(8,128)S(1)} %gather_fusion, f32[64]{0:T(128)S(1)} %compare_convert_fusion.2, pred[64]{0:T(512)(128)(4,1)S(1)} %get-tuple-element.144), kind=kOutput, calls=%fused_computation.3.clone.1 | convolution fusion | flops 50528256 | bytes 1835328 | tf_op jit(solution)/shard_map/while/body/tab,trb->tra/dot_general | solution.py:62
  331.4 4.4 %constant_dynamic-slice_fusion.2 = f32[64,1,4096]{2,1,0:T(1,128)S(1)} fusion(f32[64,8,4096]{2,1,0:T(8,128)} %get-tuple-element.170, s32[]{:T(128)S(6)} %select_n.43), kind=kLoop, calls=%fused_computation.11.clone.1 | loop fusion | bytes 2097156 | tf_op jit(solution)/shard_map/while/body/jit(dynamic_index_in_dim)/dynamic_slice | solution.py:58
  336.4 0.8 reshape.124
  337.3 2.0 gather_fusion
  339.3 5.3 %fusion.45 = f32[64,16,64]{2,1,0:T(8,128)} fusion(f32[64,16,64]{2,1,0:T(8,128)} %get-tuple-element.156, f32[64,64,64]{2,1,0:T(8,128)S(1)} %reshape.124, f32[64,16,64]{2,1,0:T(8,128)S(1)} %gather_fusion, f32[64]{0:T(128)S(1)} %compare_convert_fusion.2, pred[64]{0:T(512)(128)(4,1)S(1)} %get-tuple-element.144), kind=kOutput, calls=%fused_computation.3.clone.1 | convolution fusion | flops 50528256 | bytes 1835328 | tf_op jit(solution)/shard_map/while/body/tab,trb->tra/dot_general | solution.py:62
  345.2 4.4 %constant_dynamic-slice_fusion.2 = f32[64,1,4096]{2,1,0:T(1,128)S(1)} fusion(f32[64,8,4096]{2,1,0:T(8,128)} %get-tuple-element.170, s32[]{:T(128)S(6)} %select_n.43), kind=kLoop, calls=%fused_computation.11.clone.1 | loop fusion | bytes 2097156 | tf_op jit(solution)/shard_map/while/body/jit(dynamic_index_in_dim)/dynamic_slice | solution.py:58
  350.2 0.8 reshape.124
  351.1 2.0 gather_fusion
  353.1 5.3 %fusion.45 = f32[64,16,64]{2,1,0:T(8,128)} fusion(f32[64,16,64]{2,1,0:T(8,128)} %get-tuple-element.156, f32[64,64,64]{2,1,0:T(8,128)S(1)} %reshape.124, f32[64,16,64]{2,1,0:T(8,128)S(1)} %gather_fusion, f32[64]{0:T(128)S(1)} %compare_convert_fusion.2, pred[64]{0:T(512)(128)(4,1)S(1)} %get-tuple-element.144), kind=kOutput, calls=%fused_computation.3.clone.1 | convolution fusion | flops 50528256 | bytes 1835328 | tf_op jit(solution)/shard_map/while/body/tab,trb->tra/dot_general | solution.py:62
  359.0 4.4 %constant_dynamic-slice_fusion.2 = f32[64,1,4096]{2,1,0:T(1,128)S(1)} fusion(f32[64,8,4096]{2,1,0:T(8,128)} %get-tuple-element.170, s32[]{:T(128)S(6)} %select_n.43), kind=kLoop, calls=%fused_computation.11.clone.1 | loop fusion | bytes 2097156 | tf_op jit(solution)/shard_map/while/body/jit(dynamic_index_in_dim)/dynamic_slice | solution.py:58
  364.0 0.8 reshape.124
  364.9 2.0 gather_fusion
  366.9 5.3 %fusion.45 = f32[64,16,64]{2,1,0:T(8,128)} fusion(f32[64,16,64]{2,1,0:T(8,128)} %get-tuple-element.156, f32[64,64,64]{2,1,0:T(8,128)S(1)} %reshape.124, f32[64,16,64]{2,1,0:T(8,128)S(1)} %gather_fusion, f32[64]{0:T(128)S(1)} %compare_convert_fusion.2, pred[64]{0:T(512)(128)(4,1)S(1)} %get-tuple-element.144), kind=kOutput, calls=%fused_computation.3.clone.1 | convolution fusion | flops 50528256 | bytes 1835328 | tf_op jit(solution)/shard_map/while/body/tab,trb->tra/dot_general | solution.py:62
  372.7 2.6 fusion.13
  375.5 0.9 reshape.86
  (79 shorter events, 9.0 us)
Async XLA Ops:
  0.0 15.8 %copy-start.2 = (f32[64,1024]{1,0:T(8,128)S(1)}, f32[64,1024]{1,0:T(8,128)}, u32[]{:S(2)}) copy-start(f32[64,1024]{1,0:T(8,128)} %param.21) | copy-start | bytes 786436
  0.0 257.1 %collective-permute-start.1 = (f32[16,4096]{1,0:T(8,128)}, f32[16,4096]{1,0:T(8,128)S(1)}, u32[]{:S(2)}, u32[]{:S(2)}) collective-permute-start(f32[16,4096]{1,0:T(8,128)} %param.14), channel_id=1, source_target_pairs={{1,0},{2,1},{3,2},{4,3},{5,4},{6,5},{7,6},{8,7},{9,8},{10,9},{11,1... | collective-permute-start | bytes 786440 | tf_op jit(solution)/shard_map/ppermute | solution.py:22
  1.4 255.7 %collective-permute-start = (f32[16,4096]{1,0:T(8,128)}, f32[16,4096]{1,0:T(8,128)}, u32[]{:S(2)}, u32[]{:S(2)}) collective-permute-start(f32[16,4096]{1,0:T(8,128)} %param.14), channel_id=1, source_target_pairs={{0,1},{1,2},{2,3},{3,4},{4,5},{5,6},{6,7},{7,8},{8,9},{9,10},{10,1... | collective-permute-start | bytes 786440 | tf_op jit(solution)/shard_map/ppermute | solution.py:21
  7.8 71.4 %copy-start = (f32[64,32,64]{2,1,0:T(8,128)}, f32[64,32,64]{2,1,0:T(8,128)S(1)}, u32[]{:S(2)}) copy-start(f32[64,32,64]{2,1,0:T(8,128)S(1)} %reshape.72) | copy-start | bytes 1572868
  9.7 70.4 %copy-start.7 = (s32[4,8]{1,0:T(4,128)S(1)}, s32[4,8]{1,0:T(4,128)}, u32[]{:S(2)}) copy-start(s32[4,8]{1,0:T(4,128)} %param.22) | copy-start | bytes 388
  9.9 72.9 %copy-start.3 = (f32[4,1024]{1,0:T(4,128)S(1)}, f32[4,1024]{1,0:T(4,128)}, u32[]{:S(2)}) copy-start(f32[4,1024]{1,0:T(4,128)} %param.24) | copy-start | bytes 49156
  9.9 211.4 %copy-start.4 = (f32[1,4,1024]{2,1,0:T(4,128)S(1)}, f32[1,4,1024]{2,1,0:T(4,128)}, u32[]{:S(2)}) copy-start(f32[1,4,1024]{2,1,0:T(4,128)} %param.25) | copy-start | bytes 49156
  10.0 211.4 %copy-start.5 = (s32[64,8]{0,1:T(8,128)S(1)}, s32[64,8]{0,1:T(8,128)}, u32[]{:S(2)}) copy-start(s32[64,8]{0,1:T(8,128)} %param.19) | copy-start | bytes 6148
  10.9 225.9 %collective-permute-start.3 = (f32[16,2048]{1,0:T(8,128)}, f32[16,2048]{1,0:T(8,128)}, u32[]{:S(2)}, u32[]{:S(2)}) collective-permute-start(f32[16,2048]{1,0:T(8,128)} %reshape.74), channel_id=1, source_target_pairs={{1,0},{2,1},{3,2},{4,3},{5,4},{6,5},{7,6},{8,7},{9,8},{10,9},{11,1... | collective-permute-start | bytes 393224 | tf_op jit(solution)/shard_map/ppermute | solution.py:22
  12.2 226.9 %collective-permute-start.2 = (f32[16,2048]{1,0:T(8,128)}, f32[16,2048]{1,0:T(8,128)}, u32[]{:S(2)}, u32[]{:S(2)}) collective-permute-start(f32[16,2048]{1,0:T(8,128)} %reshape.74), channel_id=1, source_target_pairs={{0,1},{1,2},{2,3},{3,4},{4,5},{5,6},{6,7},{7,8},{8,9},{9,10},{10,1... | collective-permute-start | bytes 393224 | tf_op jit(solution)/shard_map/ppermute | solution.py:21
  16.0 206.8 %copy-start.6 = (s32[64,8]{0,1:T(8,128)S(1)}, s32[64,8]{0,1:T(8,128)}, u32[]{:S(2)}) copy-start(s32[64,8]{0,1:T(8,128)} %param.16) | copy-start | bytes 6148
  226.7 9.4 %copy-start.8 = (s32[64]{0:T(128)S(1)}, s32[64]{0:T(128)}, u32[]{:S(2)}) copy-start(s32[64]{0:T(128)} %param.17) | copy-start | bytes 772
  244.6 12.5 %copy-start.1 = (f32[16,4096]{1,0:T(8,128)S(1)}, f32[16,4096]{1,0:T(8,128)}, u32[]{:S(2)}) copy-start(f32[16,4096]{1,0:T(8,128)} %param.14) | copy-start | bytes 786436
where the time goes:
time: 378 us; the launch traced here: 376 us
  blocking collectives  198 us (52%)
  local copies, waits for them, and re-layouts  95.3 us (25%)
  matrix products  63.6 us (17%)
  starting transfers between devices  10.1 us (3%)
  loops' own time  5.86 us (2%)
    psum x1, blocking collectives, per_device(): group_sum = lax.psum(projected_sum, 'leaf')  127 us
    all_gather x1, blocking collectives, per_device(): shard_rows = lax.all_gather(cluster_rows, 'leaf', axis=0, tiled=True)  60.3 us
    dot_general x8, matrix products, near_step(): term = jnp.einsum('tab,trb->tra', slab, picked, precision=highest_precision)  42 us
    dynamic_slice x16, local copies, waits for them, and re-layouts, near_step(): lax.dynamic_index_in_dim(near_blocks, slot_index, axis=1, keepdims=False)  40.3 us
    gather x8, local copies, waits for them, and re-layouts, near_step(): picked = jnp.take(point_blocks, near_local[:, slot_index], axis=0)  16 us
    all_gather x1, blocking collectives, per_device(): all_groups = lax.all_gather(group_sum, 'group', axis=0, tiled=True)  11.2 us
    dot_general x1, matrix products, per_device(): jnp.einsum('tjkl,rtjl->tkr', leaf_coupling.reshape(leaves_here, FAR0, K,...  10.6 us
    reshape x1, local copies, waits for them, and re-layouts, per_device(): leaf_coupling.reshape(leaves_here, FAR0, K, K)  9.12 us
  transfers between devices with their start and end apart: 4, of which 0 were waited for; matrix products, arithmetic and copies ran while one was open for 13% of the time, Pallas kernels for 0%

commit v1 on v0

--- a/solution.py
+++ b/solution.py
@@ -9,6 +9,18 @@
 FAR0 = 8
 FAR1 = 8
 highest_precision = lax.Precision.HIGHEST
+
+
+def switch_frame(message, dim_k):
+    return jnp.concatenate(
+        lax.all_to_all(
+            jnp.stack([message] * lax.axis_size("leaf")),
+            axis_name="leaf",
+            split_axis=0,
+            concat_axis=0,
+        ),
+        dim_k,
+    )
 
 
 def extended(value, sides, width):
@@ -78,7 +90,7 @@
     cluster_coef = lifted.reshape(clusters_here, leaves_here // clusters_here, K, RHS).sum(axis=1)
     cluster_rows = cluster_coef.reshape(clusters_here, K * RHS)
     couplings = cluster_coupling.reshape(clusters_here, FAR1, K, K)
-    shard_rows = lax.all_gather(cluster_rows, "leaf", axis=0, tiled=True)
+    shard_rows = switch_frame(cluster_rows, dim_k=0)
     onehot = (cluster_source[:, :, None] == jnp.arange(shard_rows.shape[0])[None, None, :]).astype(
         jnp.float32
     )

time: 378 us -> 344 us (0.910)
  blocking collectives: 198 us -> 142 us
  starting transfers between devices: 10.1 us -> 28.3 us
    all_gather x1 -> x0, blocking collectives: 60.3 us -> none  [per_device(): shard_rows = lax.all_gather(cluster_rows, 'leaf', axis=0, tiled=True)]
    all_to_all x0 -> x1, starting transfers between devices: none -> 18.1 us  [switch_frame(): lax.all_to_all(jnp.stack([message] * lax.axis_size('leaf')), axis_name='l...]
    psum x1, blocking collectives: 127 us -> 131 us  [per_device(): group_sum = lax.psum(projected_sum, 'leaf')]
  transfers between devices with their start and end apart: 4 -> 5, of which waited for: 0 -> 0; matrix products, arithmetic and copies ran while one was open for 13% -> 45% of each run, Pallas kernels for 0% -> 0%
where the time goes in v1:
time: 344 us; the launch traced here: 341 us
  blocking collectives  142 us (41%)
  local copies, waits for them, and re-layouts  98.4 us (29%)
  matrix products  63.5 us (18%)
  starting transfers between devices  28.3 us (8%)
  loops' own time  5.99 us (2%)
    psum x1, blocking collectives, per_device(): group_sum = lax.psum(projected_sum, 'leaf')  131 us
    dot_general x8, matrix products, near_step(): term = jnp.einsum('tab,trb->tra', slab, picked, precision=highest_precision)  42.1 us
    dynamic_slice x16, local copies, waits for them, and re-layouts, near_step(): lax.dynamic_index_in_dim(near_blocks, slot_index, axis=1, keepdims=False)  40.3 us
    all_to_all x1, starting transfers between devices, switch_frame(): lax.all_to_all(jnp.stack([message] * lax.axis_size('leaf')), axis_name='l...  18.1 us
    gather x8, local copies, waits for them, and re-layouts, near_step(): picked = jnp.take(point_blocks, near_local[:, slot_index], axis=0)  16 us
    dot_general x1, matrix products, per_device(): jnp.einsum('tjkl,rtjl->tkr', leaf_coupling.reshape(leaves_here, FAR0, K,...  11.4 us
    all_gather x1, blocking collectives, per_device(): all_groups = lax.all_gather(group_sum, 'group', axis=0, tiled=True)  11.2 us
    reshape x1, local copies, waits for them, and re-layouts, per_device(): leaf_coupling.reshape(leaves_here, FAR0, K, K)  9.15 us
  transfers between devices with their start and end apart: 5, of which 0 were waited for; matrix products, arithmetic and copies ran while one was open for 45% of the time, Pallas kernels for 0%

profile of v1, /device:TPU:0, one launch (start us, length us, event | category | flops | bytes accessed | tf_op | source)
XLA Modules:
  0.0 340.6 jit_solution(17616240980550156632)
XLA Ops:
  0.0 1.4 collective-permute-start.1
  1.4 3.8 %collective-permute-start = (f32[16,4096]{1,0:T(8,128)}, f32[16,4096]{1,0:T(8,128)}, u32[]{:S(2)}, u32[]{:S(2)}) collective-permute-start(f32[16,4096]{1,0:T(8,128)} %param.14), channel_id=1, source_target_pairs={{0,1},{1,2},{2,3},{3,4},{4,5},{5,6},{6,7},{7,8},{8,9},{9,10},{10,1... | collective-permute-start | bytes 786440 | tf_op jit(solution)/shard_map/ppermute | solution.py:33
  5.2 1.1 reshape.74
  6.3 1.5 reshape.73
  7.8 2.0 fusion.17
  10.0 0.9 reshape.75
  10.9 1.3 collective-permute-start.3
  12.2 3.7 %collective-permute-start.2 = (f32[16,2048]{1,0:T(8,128)}, f32[16,2048]{1,0:T(8,128)}, u32[]{:S(2)}, u32[]{:S(2)}) collective-permute-start(f32[16,2048]{1,0:T(8,128)} %reshape.75), channel_id=1, source_target_pairs={{0,1},{1,2},{2,3},{3,4},{4,5},{5,6},{6,7},{7,8},{8,9},{9,10},{10,1... | collective-permute-start | bytes 393224 | tf_op jit(solution)/shard_map/ppermute | solution.py:33
  16.1 0.9 copy.108
  17.0 1.7 bitcast_reduce_fusion
  18.9 0.9 stack.3
  19.9 18.1 %all-to-all-start = ((f32[64,4,512]{2,1,0:T(4,128)}), f32[64,4,512]{2,1,0:T(4,128)}, u32[]{:S(2)}, u32[]{:S(2)}) async-start(f32[64,4,512]{2,1,0:T(4,128)} %stack.3), calls=%async_computation | async-start | bytes 1048576 | tf_op jit(solution)/shard_map/all_to_all | solution.py:16
  38.4 130.9 %psum.7 = f32[1,512]{1,0:T(1,128)S(1)} all-reduce(f32[1,512]{1,0:T(1,128)S(1)} %reshape.82), channel_id=1, replica_groups=mesh['group'=4,'leaf'=64] {'leaf'}, use_global_device_ids=true, to_apply=%region_4.5 | all-reduce | flops 512 | bytes 4096 | tf_op jit(solution)/shard_map/psum | solution.py:103
  169.3 11.2 %all-gather = f32[4,1,512]{2,1,0:T(1,128)S(1)} all-gather(f32[1,1,512]{2,1,0:T(1,128)S(1)} %bitcast.85), channel_id=1, replica_groups=mesh['group'=4,'leaf'=64] {'group'}, dimensions={0}, use_global_device_ids=true | all-gather | bytes 10240 | tf_op jit(solution)/shard_map/all_gather | solution.py:104
  181.0 3.8 %copy.105 = f32[64,8,1024]{0,2,1:T(8,128)} copy(f32[64,8,1024]{2,1,0:T(8,128)} %param.20) | data formatting | bytes 4194304 | tf_op args[6]
  184.9 9.2 %copy.106 = f32[64,8,32,32]{3,2,1,0:T(8,128)} copy(f32[64,8,32,32]{0,3,2,1:T(8,128)} %bitcast.75) | data formatting | bytes 4194304 | tf_op jit(solution)/shard_map/reshape | solution.py:84
  194.3 1.0 reshape.80
  196.0 1.1 concatenate.13
  197.4 1.1 concatenate.12
  198.9 3.1 gather_fusion.1
  202.0 11.4 %fusion.10 = f32[64,16,32]{2,1,0:T(8,128)} fusion(f32[64,8,32,32]{3,2,1,0:T(8,128)} %copy.106, f32[64,8,16,32]{3,2,1,0:T(8,128)} %bitcast.76, pred[64,8]{1,0:T(8,128)(4,1)S(1)} %copy.99), kind=kOutput, calls=%fused_computation.19 | convolution fusion | flops 100925440 | bytes 3277312 | tf_op jit(solution)/shard_map/tjkl,rtjl->tkr/dot_general | solution.py:82
  213.4 1.0 pad_maximum_fusion.1
  215.0 2.1 copy.97
  217.1 0.8 broadcast_in_dim.31
  218.0 111.3 %while.10 = (s32[]{:T(128)}, f32[64,16,64]{2,1,0:T(8,128)}, s32[]{:T(128)}, s32[64,8]{0,1:T(8,128)S(1)}, f32[192,16,64]{2,1,0:T(8,128)}, /*index=5*/f32[64,8,409...) while((s32[]{:T(128)}, f32[64,16,64]{2,1,0:T(8,128)}, s32[]{:T(128)}, ...), condition=%wide.region_2.0_spmd, body=%wide.region_1.2_spmd.sunk | while | flops 50529796 | bytes 8656923 | solution.py:77
  218.8 4.4 %constant_dynamic-slice_fusion.2 = f32[64,1,4096]{2,1,0:T(1,128)S(1)} fusion(f32[64,8,4096]{2,1,0:T(8,128)} %get-tuple-element.177, s32[]{:T(128)S(6)} %select_n.43), kind=kLoop, calls=%fused_computation.11.clone.1 | loop fusion | bytes 2097156 | tf_op jit(solution)/shard_map/while/body/jit(dynamic_index_in_dim)/dynamic_slice | solution.py:70
  223.9 0.8 reshape.121
  224.7 2.0 gather_fusion
  226.8 5.3 %fusion.48 = f32[64,16,64]{2,1,0:T(8,128)} fusion(f32[64,16,64]{2,1,0:T(8,128)} %get-tuple-element.163, f32[64,64,64]{2,1,0:T(8,128)S(1)} %reshape.121, f32[64,16,64]{2,1,0:T(8,128)S(1)} %gather_fusion, f32[64]{0:T(128)S(1)} %compare_convert_fusion.2, pred[64]{0:T(512)(128)(4,1)S(1)} %get-tuple-element.151), kind=kOutput, calls=%fused_computation.3.clone.1 | convolution fusion | flops 50528256 | bytes 1835328 | tf_op jit(solution)/shard_map/while/body/tab,trb->tra/dot_general | solution.py:74
  232.6 4.4 %constant_dynamic-slice_fusion.2 = f32[64,1,4096]{2,1,0:T(1,128)S(1)} fusion(f32[64,8,4096]{2,1,0:T(8,128)} %get-tuple-element.177, s32[]{:T(128)S(6)} %select_n.43), kind=kLoop, calls=%fused_computation.11.clone.1 | loop fusion | bytes 2097156 | tf_op jit(solution)/shard_map/while/body/jit(dynamic_index_in_dim)/dynamic_slice | solution.py:70
  237.7 0.8 reshape.121
  238.6 2.0 gather_fusion
  240.6 5.3 %fusion.48 = f32[64,16,64]{2,1,0:T(8,128)} fusion(f32[64,16,64]{2,1,0:T(8,128)} %get-tuple-element.163, f32[64,64,64]{2,1,0:T(8,128)S(1)} %reshape.121, f32[64,16,64]{2,1,0:T(8,128)S(1)} %gather_fusion, f32[64]{0:T(128)S(1)} %compare_convert_fusion.2, pred[64]{0:T(512)(128)(4,1)S(1)} %get-tuple-element.151), kind=kOutput, calls=%fused_computation.3.clone.1 | convolution fusion | flops 50528256 | bytes 1835328 | tf_op jit(solution)/shard_map/while/body/tab,trb->tra/dot_general | solution.py:74
  246.4 4.4 %constant_dynamic-slice_fusion.2 = f32[64,1,4096]{2,1,0:T(1,128)S(1)} fusion(f32[64,8,4096]{2,1,0:T(8,128)} %get-tuple-element.177, s32[]{:T(128)S(6)} %select_n.43), kind=kLoop, calls=%fused_computation.11.clone.1 | loop fusion | bytes 2097156 | tf_op jit(solution)/shard_map/while/body/jit(dynamic_index_in_dim)/dynamic_slice | solution.py:70
  251.5 0.8 reshape.121
  252.4 2.0 gather_fusion
  254.4 5.3 %fusion.48 = f32[64,16,64]{2,1,0:T(8,128)} fusion(f32[64,16,64]{2,1,0:T(8,128)} %get-tuple-element.163, f32[64,64,64]{2,1,0:T(8,128)S(1)} %reshape.121, f32[64,16,64]{2,1,0:T(8,128)S(1)} %gather_fusion, f32[64]{0:T(128)S(1)} %compare_convert_fusion.2, pred[64]{0:T(512)(128)(4,1)S(1)} %get-tuple-element.151), kind=kOutput, calls=%fused_computation.3.clone.1 | convolution fusion | flops 50528256 | bytes 1835328 | tf_op jit(solution)/shard_map/while/body/tab,trb->tra/dot_general | solution.py:74
  260.3 4.4 %constant_dynamic-slice_fusion.2 = f32[64,1,4096]{2,1,0:T(1,128)S(1)} fusion(f32[64,8,4096]{2,1,0:T(8,128)} %get-tuple-element.177, s32[]{:T(128)S(6)} %select_n.43), kind=kLoop, calls=%fused_computation.11.clone.1 | loop fusion | bytes 2097156 | tf_op jit(solution)/shard_map/while/body/jit(dynamic_index_in_dim)/dynamic_slice | solution.py:70
  265.3 0.8 reshape.121
  266.2 2.0 gather_fusion
  268.2 5.3 %fusion.48 = f32[64,16,64]{2,1,0:T(8,128)} fusion(f32[64,16,64]{2,1,0:T(8,128)} %get-tuple-element.163, f32[64,64,64]{2,1,0:T(8,128)S(1)} %reshape.121, f32[64,16,64]{2,1,0:T(8,128)S(1)} %gather_fusion, f32[64]{0:T(128)S(1)} %compare_convert_fusion.2, pred[64]{0:T(512)(128)(4,1)S(1)} %get-tuple-element.151), kind=kOutput, calls=%fused_computation.3.clone.1 | convolution fusion | flops 50528256 | bytes 1835328 | tf_op jit(solution)/shard_map/while/body/tab,trb->tra/dot_general | solution.py:74
  274.1 4.4 %constant_dynamic-slice_fusion.2 = f32[64,1,4096]{2,1,0:T(1,128)S(1)} fusion(f32[64,8,4096]{2,1,0:T(8,128)} %get-tuple-element.177, s32[]{:T(128)S(6)} %select_n.43), kind=kLoop, calls=%fused_computation.11.clone.1 | loop fusion | bytes 2097156 | tf_op jit(solution)/shard_map/while/body/jit(dynamic_index_in_dim)/dynamic_slice | solution.py:70
  279.1 0.8 reshape.121
  280.0 2.0 gather_fusion
  282.0 5.3 %fusion.48 = f32[64,16,64]{2,1,0:T(8,128)} fusion(f32[64,16,64]{2,1,0:T(8,128)} %get-tuple-element.163, f32[64,64,64]{2,1,0:T(8,128)S(1)} %reshape.121, f32[64,16,64]{2,1,0:T(8,128)S(1)} %gather_fusion, f32[64]{0:T(128)S(1)} %compare_convert_fusion.2, pred[64]{0:T(512)(128)(4,1)S(1)} %get-tuple-element.151), kind=kOutput, calls=%fused_computation.3.clone.1 | convolution fusion | flops 50528256 | bytes 1835328 | tf_op jit(solution)/shard_map/while/body/tab,trb->tra/dot_general | solution.py:74
  287.9 4.4 %constant_dynamic-slice_fusion.2 = f32[64,1,4096]{2,1,0:T(1,128)S(1)} fusion(f32[64,8,4096]{2,1,0:T(8,128)} %get-tuple-element.177, s32[]{:T(128)S(6)} %select_n.43), kind=kLoop, calls=%fused_computation.11.clone.1 | loop fusion | bytes 2097156 | tf_op jit(solution)/shard_map/while/body/jit(dynamic_index_in_dim)/dynamic_slice | solution.py:70
  292.9 0.8 reshape.121
  293.8 2.0 gather_fusion
  295.8 5.3 %fusion.48 = f32[64,16,64]{2,1,0:T(8,128)} fusion(f32[64,16,64]{2,1,0:T(8,128)} %get-tuple-element.163, f32[64,64,64]{2,1,0:T(8,128)S(1)} %reshape.121, f32[64,16,64]{2,1,0:T(8,128)S(1)} %gather_fusion, f32[64]{0:T(128)S(1)} %compare_convert_fusion.2, pred[64]{0:T(512)(128)(4,1)S(1)} %get-tuple-element.151), kind=kOutput, calls=%fused_computation.3.clone.1 | convolution fusion | flops 50528256 | bytes 1835328 | tf_op jit(solution)/shard_map/while/body/tab,trb->tra/dot_general | solution.py:74
  301.7 4.4 %constant_dynamic-slice_fusion.2 = f32[64,1,4096]{2,1,0:T(1,128)S(1)} fusion(f32[64,8,4096]{2,1,0:T(8,128)} %get-tuple-element.177, s32[]{:T(128)S(6)} %select_n.43), kind=kLoop, calls=%fused_computation.11.clone.1 | loop fusion | bytes 2097156 | tf_op jit(solution)/shard_map/while/body/jit(dynamic_index_in_dim)/dynamic_slice | solution.py:70
  306.8 0.8 reshape.121
  307.6 2.0 gather_fusion
  309.7 5.3 %fusion.48 = f32[64,16,64]{2,1,0:T(8,128)} fusion(f32[64,16,64]{2,1,0:T(8,128)} %get-tuple-element.163, f32[64,64,64]{2,1,0:T(8,128)S(1)} %reshape.121, f32[64,16,64]{2,1,0:T(8,128)S(1)} %gather_fusion, f32[64]{0:T(128)S(1)} %compare_convert_fusion.2, pred[64]{0:T(512)(128)(4,1)S(1)} %get-tuple-element.151), kind=kOutput, calls=%fused_computation.3.clone.1 | convolution fusion | flops 50528256 | bytes 1835328 | tf_op jit(solution)/shard_map/while/body/tab,trb->tra/dot_general | solution.py:74
  315.5 4.4 %constant_dynamic-slice_fusion.2 = f32[64,1,4096]{2,1,0:T(1,128)S(1)} fusion(f32[64,8,4096]{2,1,0:T(8,128)} %get-tuple-element.177, s32[]{:T(128)S(6)} %select_n.43), kind=kLoop, calls=%fused_computation.11.clone.1 | loop fusion | bytes 2097156 | tf_op jit(solution)/shard_map/while/body/jit(dynamic_index_in_dim)/dynamic_slice | solution.py:70
  320.6 0.8 reshape.121
  321.5 2.0 gather_fusion
  323.5 5.3 %fusion.48 = f32[64,16,64]{2,1,0:T(8,128)} fusion(f32[64,16,64]{2,1,0:T(8,128)} %get-tuple-element.163, f32[64,64,64]{2,1,0:T(8,128)S(1)} %reshape.121, f32[64,16,64]{2,1,0:T(8,128)S(1)} %gather_fusion, f32[64]{0:T(128)S(1)} %compare_convert_fusion.2, pred[64]{0:T(512)(128)(4,1)S(1)} %get-tuple-element.151), kind=kOutput, calls=%fused_computation.3.clone.1 | convolution fusion | flops 50528256 | bytes 1835328 | tf_op jit(solution)/shard_map/while/body/tab,trb->tra/dot_general | solution.py:74
  329.4 2.2 reshape.79
  331.6 2.0 copy.110
  333.6 1.9 fusion.15
  335.6 1.6 convolution_bitcast_fusion.1
  337.4 1.0 convolution_add_fusion.1
  338.5 1.0 fusion.13
  339.7 0.9 reshape.86
  (93 shorter events, 9.2 us)
Async XLA Ops:
  0.0 15.9 %copy-start.7 = (f32[64,1024]{1,0:T(8,128)S(1)}, f32[64,1024]{1,0:T(8,128)}, u32[]{:S(2)}) copy-start(f32[64,1024]{1,0:T(8,128)} %param.21) | copy-start | bytes 786436
  0.0 213.4 %collective-permute-start.1 = (f32[16,4096]{1,0:T(8,128)}, f32[16,4096]{1,0:T(8,128)S(1)}, u32[]{:S(2)}, u32[]{:S(2)}) collective-permute-start(f32[16,4096]{1,0:T(8,128)} %param.14), channel_id=1, source_target_pairs={{1,0},{2,1},{3,2},{4,3},{5,4},{6,5},{7,6},{8,7},{9,8},{10,9},{11,1... | collective-permute-start | bytes 786440 | tf_op jit(solution)/shard_map/ppermute | solution.py:34
  1.4 212.0 %collective-permute-start = (f32[16,4096]{1,0:T(8,128)}, f32[16,4096]{1,0:T(8,128)}, u32[]{:S(2)}, u32[]{:S(2)}) collective-permute-start(f32[16,4096]{1,0:T(8,128)} %param.14), channel_id=1, source_target_pairs={{0,1},{1,2},{2,3},{3,4},{4,5},{5,6},{6,7},{7,8},{8,9},{9,10},{10,1... | collective-permute-start | bytes 786440 | tf_op jit(solution)/shard_map/ppermute | solution.py:33
  7.8 12.1 %copy-start.1 = (f32[64,32,64]{2,1,0:T(8,128)}, f32[64,32,64]{2,1,0:T(8,128)S(1)}, u32[]{:S(2)}) copy-start(f32[64,32,64]{2,1,0:T(8,128)S(1)} %reshape.73) | copy-start | bytes 1572868
  9.8 28.2 %copy-start.9 = (f32[4,1024]{1,0:T(4,128)S(1)}, f32[4,1024]{1,0:T(4,128)}, u32[]{:S(2)}) copy-start(f32[4,1024]{1,0:T(4,128)} %param.24) | copy-start | bytes 49156
  9.8 170.9 %copy-start.10 = (f32[1,4,1024]{2,1,0:T(4,128)S(1)}, f32[1,4,1024]{2,1,0:T(4,128)}, u32[]{:S(2)}) copy-start(f32[1,4,1024]{2,1,0:T(4,128)} %param.25) | copy-start | bytes 49156
  9.8 171.0 %copy-start.11 = (s32[64,8]{0,1:T(8,128)S(1)}, s32[64,8]{0,1:T(8,128)}, u32[]{:S(2)}) copy-start(s32[64,8]{0,1:T(8,128)} %param.19) | copy-start | bytes 6148
  9.8 171.2 %copy-start.12 = (s32[64,8]{0,1:T(8,128)S(1)}, s32[64,8]{0,1:T(8,128)}, u32[]{:S(2)}) copy-start(s32[64,8]{0,1:T(8,128)} %param.16) | copy-start | bytes 6148
  10.9 185.1 %collective-permute-start.3 = (f32[16,2048]{1,0:T(8,128)}, f32[16,2048]{1,0:T(8,128)}, u32[]{:S(2)}, u32[]{:S(2)}) collective-permute-start(f32[16,2048]{1,0:T(8,128)} %reshape.75), channel_id=1, source_target_pairs={{1,0},{2,1},{3,2},{4,3},{5,4},{6,5},{7,6},{8,7},{9,8},{10,9},{11,1... | collective-permute-start | bytes 393224 | tf_op jit(solution)/shard_map/ppermute | solution.py:34
  12.2 185.2 %collective-permute-start.2 = (f32[16,2048]{1,0:T(8,128)}, f32[16,2048]{1,0:T(8,128)}, u32[]{:S(2)}, u32[]{:S(2)}) collective-permute-start(f32[16,2048]{1,0:T(8,128)} %reshape.75), channel_id=1, source_target_pairs={{0,1},{1,2},{2,3},{3,4},{4,5},{5,6},{6,7},{7,8},{8,9},{9,10},{10,1... | collective-permute-start | bytes 393224 | tf_op jit(solution)/shard_map/ppermute | solution.py:33
  17.0 167.9 %copy-start.3 = (f32[64,32,32]{2,1,0:T(8,128)}, f32[64,32,32]{2,1,0:T(8,128)S(1)}, u32[]{:S(2)}) copy-start(f32[64,32,32]{2,1,0:T(8,128)S(1)} %copy.108) | copy-start | bytes 786436
  19.9 309.5 %all-to-all-start = ((f32[64,4,512]{2,1,0:T(4,128)}), f32[64,4,512]{2,1,0:T(4,128)}, u32[]{:S(2)}, u32[]{:S(2)}) async-start(f32[64,4,512]{2,1,0:T(4,128)} %stack.3), calls=%async_computation | async-start | bytes 1048576 | tf_op jit(solution)/shard_map/all_to_all | solution.py:16
  184.9 9.4 %copy-start.8 = (f32[4,8,1024]{2,1,0:T(8,128)S(1)}, f32[4,8,1024]{2,1,0:T(8,128)}, u32[]{:S(2)}) copy-start(f32[4,8,1024]{2,1,0:T(8,128)} %param.23) | copy-start | bytes 393220
  184.9 10.4 %copy-start.14 = (s32[64]{0:T(128)S(1)}, s32[64]{0:T(128)}, u32[]{:S(2)}) copy-start(s32[64]{0:T(128)} %param.17) | copy-start | bytes 772
  202.0 11.5 %copy-start.6 = (f32[16,4096]{1,0:T(8,128)S(1)}, f32[16,4096]{1,0:T(8,128)}, u32[]{:S(2)}) copy-start(f32[16,4096]{1,0:T(8,128)} %param.14) | copy-start | bytes 786436
  218.0 115.6 %copy-start.13 = (s32[4,8]{1,0:T(4,128)S(1)}, s32[4,8]{1,0:T(4,128)}, u32[]{:S(2)}) copy-start(s32[4,8]{1,0:T(4,128)} %param.22) | copy-start | bytes 388
  329.3 8.1 %copy-start.4 = (f32[64,32,32]{2,1,0:T(8,128)S(1)}, f32[64,32,32]{2,1,0:T(8,128)}, u32[]{:S(2)}) copy-start(f32[64,32,32]{2,1,0:T(8,128)} %copy-done.3) | copy-start | bytes 786436
  329.3 8.1 %copy-start.5 = (f32[64,16,32]{2,1,0:T(8,128)S(1)}, f32[64,16,32]{2,1,0:T(8,128)}, u32[]{:S(2)}) copy-start(f32[64,16,32]{2,1,0:T(8,128)} %fusion.10) | copy-start | bytes 393220
  329.4 9.1 %copy-start = (f32[64,16,64]{2,1,0:T(8,128)S(1)}, f32[64,16,64]{2,1,0:T(8,128)}, u32[]{:S(2)}) copy-start(f32[64,16,64]{2,1,0:T(8,128)} %get-tuple-element.43) | copy-start | bytes 786436
  329.4 9.1 %copy-start.2 = (f32[64,32,64]{2,1,0:T(8,128)S(1)}, f32[64,32,64]{2,1,0:T(8,128)}, u32[]{:S(2)}) copy-start(f32[64,32,64]{2,1,0:T(8,128)} %copy-done.1) | copy-start | bytes 1572868
